TPU v7x, 128 devices: a whole 4x4x4 slice. The times are simulated.
128 devices in a mesh: req: 64 (over y, x, z), head: 2 (over core).
Axes of the slice: x: 4, y: 4, z: 4, core: 2. Of those that a mesh axis runs over, the one named last changes fastest.
Arguments:
- hidden_in: bfloat16 [4096, 2048], P('req'), may hold values from -14 to 14
- attn_gain: float32 [2048], replicated, may hold values from 0.1 to 1.9
- w_query: bfloat16 [2048, 2048], P(None, 'head'), may hold values from -0.125 to 0.125
- w_key: bfloat16 [2048, 1024], P(None, 'head'), may hold values from -0.125 to 0.125
- w_value: bfloat16 [2048, 1024], P(None, 'head'), may hold values from -0.125 to 0.125
- query_gain: float32 [128], replicated, may hold values from 0.5 to 2
- key_gain: float32 [128], replicated, may hold values from 0.5 to 2
- w_out: bfloat16 [2048, 2048], P('head'), may hold values from -0.125 to 0.125
- cache_keys: bfloat16 [64, 2048, 1024], P('req', None, 'head'), may hold values from -3.5 to 3.5
- cache_values: bfloat16 [64, 2048, 1024], P('req', None, 'head'), may hold values from -6 to 6
- cache_lengths: int32 [64], replicated, may hold values from 1 to 2048, 65536 in all
- slot_request: int32 [64], replicated, may hold values from 0 to 63, each once
- mlp_gain: float32 [2048], P('head'), may hold values from 0.1 to 1.9
- w_gate: bfloat16 [2048, 6144], P('head', 'req'), may hold values from -0.125 to 0.125
- w_up: bfloat16 [2048, 6144], P('head', 'req'), may hold values from -0.125 to 0.125
- w_down: bfloat16 [6144, 2048], P('req', 'head'), may hold values from -0.078125 to 0.078125
- final_gain: float32 [2048], replicated, may hold values from 0.1 to 1.9
- w_vocab: bfloat16 [2048, 151936], P(None, ('req', 'head')), may hold values from -8 to 8
Outputs:
- hidden_out: bfloat16 [4096, 2048], P('req', 'head')
- log_probs: float32 [64, 151936], P(None, ('req', 'head'))
Inputs may be any that keep to these rules, and one draw needn't show every extreme that they name: `cache_lengths`: the largest length is exactly 2048. `slot_request`: each request appears once.
All inputs are finite; a program needn't handle non-finite values.
Results may differ from a plain program's by a relative error of at most 0.008.
Values may be sent and summed in bfloat16 or wider, within the bound.
A program may use at most 128 MiB of HBM per device.

v0:
```python
import jax
import jax.numpy as jnp
from jax import lax
from jax.sharding import PartitionSpec as P

D = 2048
HEAD_DIM = 128
EPS = 1e-06
ROPE_BASE = 1000000.0
NEG = -1e30


def norm_rows(field, gain_vec):
    return field * lax.rsqrt(jnp.mean(field * field, axis=-1, keepdims=True) + EPS) * gain_vec


def rotate(field, positions):
    half_dim = field.shape[-1] // 2
    frequency = ROPE_BASE ** (-2.0 * jnp.arange(half_dim, dtype=jnp.float32) / field.shape[-1])
    angles = positions[..., None, None] * frequency
    cosine = jnp.cos(angles)
    sines = jnp.sin(angles)
    lower_half = field[..., :half_dim]
    upper_half = field[..., half_dim:]
    return jnp.concatenate(
        [lower_half * cosine - upper_half * sines, upper_half * cosine + lower_half * sines],
        axis=-1,
    )


def inverse_order(slot_request):
    indices = jnp.arange(slot_request.shape[0], dtype=jnp.int32)
    return jnp.sum(
        jnp.where(slot_request[None, :] == indices[:, None], indices[None, :], 0), axis=1
    )


def attend_slot(queries, keys_new, values_new, keys_cache, values_cache, cache_len):
    row_count, value_heads, head_size = keys_new.shape
    group_size = queries.shape[1] // value_heads
    grouped = queries.reshape(row_count, value_heads, group_size, head_size)
    score_scale = head_size ** (-0.5)
    recent = (
        jnp.einsum("skgd,tkd->kgst", grouped, keys_new, preferred_element_type=jnp.float32)
        * score_scale
    )
    causal = jnp.arange(row_count)[:, None] >= jnp.arange(row_count)[None, :]
    recent = jnp.where(causal, recent, NEG)
    cache_span = keys_cache.shape[0]
    stored = (
        jnp.einsum("skgd,lkd->kgsl", grouped, keys_cache, preferred_element_type=jnp.float32)
        * score_scale
    )
    stored = jnp.where(jnp.arange(cache_span, dtype=jnp.int32) < cache_len, stored, NEG)
    old_weights = jnp.exp(stored)
    new_weights = jnp.exp(recent)
    row_total = jnp.sum(old_weights, axis=-1) + jnp.sum(new_weights, axis=-1)
    old_weights = (old_weights / row_total[..., None]).astype(jnp.bfloat16)
    new_weights = (new_weights / row_total[..., None]).astype(jnp.bfloat16)
    blended = jnp.einsum(
        "kgsl,lkd->skgd", old_weights, values_cache, preferred_element_type=jnp.float32
    )
    blended = blended + jnp.einsum(
        "kgst,tkd->skgd", new_weights, values_new, preferred_element_type=jnp.float32
    )
    return blended.reshape(row_count, value_heads * group_size * head_size).astype(jnp.bfloat16)


def on_device(
    hidden_in,
    attn_gain,
    w_query,
    w_key,
    w_value,
    query_gain,
    key_gain,
    w_out,
    cache_keys,
    cache_values,
    cache_lengths,
    slot_request,
    mlp_gain,
    w_gate,
    w_up,
    w_down,
    final_gain,
    w_vocab,
):
    row_count = hidden_in.shape[0]
    half_width = mlp_gain.shape[0]
    slot_index = lax.axis_index("req")
    request_id = lax.dynamic_index_in_dim(slot_request, slot_index, 0, keepdims=False)
    cache_len = lax.dynamic_index_in_dim(cache_lengths, request_id, 0, keepdims=False)
    tokens = hidden_in.astype(jnp.float32)
    normed = norm_rows(tokens, attn_gain).astype(jnp.bfloat16)
    query_heads = w_query.shape[1] // HEAD_DIM
    value_heads = w_key.shape[1] // HEAD_DIM
    positions = (cache_len + jnp.arange(row_count, dtype=jnp.int32)).astype(jnp.float32)
    queries = jnp.dot(normed, w_query, preferred_element_type=jnp.float32).reshape(
        row_count, query_heads, HEAD_DIM
    )
    queries = rotate(norm_rows(queries, query_gain), positions).astype(jnp.bfloat16)
    keys_new = jnp.dot(normed, w_key, preferred_element_type=jnp.float32).reshape(
        row_count, value_heads, HEAD_DIM
    )
    keys_new = rotate(norm_rows(keys_new, key_gain), positions).astype(jnp.bfloat16)
    values_new = (
        jnp.dot(normed, w_value, preferred_element_type=jnp.float32)
        .astype(jnp.bfloat16)
        .reshape(row_count, value_heads, HEAD_DIM)
    )
    keys_cache = cache_keys.reshape(cache_keys.shape[1], value_heads, HEAD_DIM)
    values_cache = cache_values.reshape(cache_values.shape[1], value_heads, HEAD_DIM)
    attended = attend_slot(queries, keys_new, values_new, keys_cache, values_cache, cache_len)
    projected = jnp.dot(attended, w_out, preferred_element_type=jnp.float32)
    own_sum = lax.psum_scatter(
        projected.astype(jnp.bfloat16), "head", scatter_dimension=1, tiled=True
    ).astype(jnp.float32)
    head_part = lax.axis_index("head")
    residual = lax.dynamic_slice_in_dim(tokens, head_part * half_width, half_width, 1) + own_sum
    squares = lax.psum(jnp.sum(residual * residual, axis=1), "head")
    mixed_rows = (residual * lax.rsqrt(squares[:, None] / D + EPS) * mlp_gain).astype(jnp.bfloat16)
    paired = jnp.concatenate([w_gate, w_up], axis=1)
    partial_rows = jnp.dot(
        lax.all_gather(mixed_rows, "req", axis=0, tiled=True),
        paired,
        preferred_element_type=jnp.float32,
    )
    summed_rows = lax.psum(partial_rows.astype(jnp.bfloat16), "head").astype(jnp.float32)
    unit_count = w_gate.shape[1]
    active = (jax.nn.silu(summed_rows[:, :unit_count]) * summed_rows[:, unit_count:]).astype(
        jnp.bfloat16
    )
    down_part = lax.psum_scatter(
        jnp.dot(active, w_down, preferred_element_type=jnp.float32),
        "req",
        scatter_dimension=0,
        tiled=True,
    )
    output = residual + down_part
    hidden_out = output.astype(jnp.bfloat16)
    last_row = output[row_count - 1 :, :]
    collected = lax.all_gather(last_row, ("req", "head"), axis=1, tiled=True).reshape(-1, D)
    final_rows = norm_rows(collected, final_gain).astype(jnp.bfloat16)
    logits = jnp.dot(final_rows, w_vocab, preferred_element_type=jnp.float32)
    row_max = lax.pmax(jnp.max(logits, axis=1), ("req", "head"))
    row_total = lax.psum(jnp.sum(jnp.exp(logits - row_max[:, None]), axis=1), ("req", "head"))
    log_probs = logits - row_max[:, None] - jnp.log(row_total)[:, None]
    log_probs = jnp.take(log_probs, inverse_order(slot_request), axis=0)
    return (hidden_out, log_probs)


def solution(mesh):
    in_specs = (
        P("req", None),
        P(),
        P(None, "head"),
        P(None, "head"),
        P(None, "head"),
        P(),
        P(),
        P("head", None),
        P("req", None, "head"),
        P("req", None, "head"),
        P(),
        P(),
        P("head"),
        P("head", "req"),
        P("head", "req"),
        P("req", "head"),
        P(),
        P(None, ("req", "head")),
    )
    out_specs = (P("req", "head"), P(None, ("req", "head")))
    return jax.shard_map(
        on_device, mesh=mesh, in_specs=in_specs, out_specs=out_specs, check_vma=False
    )
```

profile of v0, /device:TPU:1, one launch (start us, length us, event | category | flops | bytes accessed | tf_op | source)
XLA Modules:
  0.0 747.4 jit_solution(8484590395757010456)
XLA Ops:
  7.2 1.4 dynamic_slice.11
  10.6 1.2 dynamic_slice.12
  11.8 0.6 add_convert_fusion.2
  12.5 0.7 iota_compare_fusion.2
  13.2 1.1 multiply_reduce_fusion.1
  14.3 3.2 convolution_bitcast_fusion
  18.5 4.0 reshape.165
  22.5 0.5 fusion.40
  23.5 4.1 reshape.167
  27.6 0.5 convolution_convert_fusion.2
  28.1 3.2 bitcast_reduce_fusion
  31.8 1.4 fusion.12
  33.7 3.8 convolution_convert_fusion.1
  37.6 14.1 %reduce-scatter.3.cloned.1.call-done = bf16[64,1024]{1,0:T(8,128)(2,1)} async-done(((bf16[64,2048]{1,0:T(8,128)(2,1)}), bf16[64,1024]{1,0:T(8,128)(2,1)}) %reduce-scatter.3.cloned.1.call-update) | async-done | bytes 131088 | tf_op jit(solution)/shard_map/reduce_scatter | solution.py:116
  51.6 1.0 multiply_reduce_fusion.2
  52.7 2.5 psum.21
  55.2 1.7 multiply_convert_fusion.3
  56.9 79.7 %all-gather.2.cloned.1.call-done = bf16[4096,1024]{1,0:T(8,128)(2,1)} async-done(((bf16[64,1024]{1,0:T(8,128)(2,1)}), bf16[4096,1024]{1,0:T(8,128)(2,1)}) %all-gather.2.cloned.1.call-update) | async-done | bytes 8388624 | tf_op jit(solution)/shard_map/all_gather | solution.py:125
  136.6 7.5 %convolution_convert_fusion = bf16[4096,192]{0,1:T(8,128)(2,1)} fusion(bf16[4096,1024]{1,0:T(8,128)(2,1)} %all-gather.2.cloned.1.call-done, bf16[1024,96]{0,1:T(8,128)(2,1)S(1)} %copy-done.12, bf16[1024,96]{0,1:T(8,128)(2,1)S(1)} %copy-done.13), kind=kOutput, calls=%fused_computation.1 | convolution fusion | flops 1612185600 | bytes 10354688 | tf_op jit(solution)/shard_map/dot_general | solution.py:124
  144.2 26.1 %all-reduce.2.cloned.1.call-done = bf16[4096,192]{0,1:T(8,128)(2,1)} async-done(((bf16[4096,192]{0,1:T(8,128)(2,1)}), bf16[4096,192]{0,1:T(8,128)(2,1)}) %all-reduce.2.cloned.1.call-update) | async-done | bytes 1572880 | tf_op jit(solution)/shard_map/psum | solution.py:129
  170.3 1.8 convert_element_type.67
  172.1 8.1 %fusion.18 = f32[4096,1024]{1,0:T(8,128)} fusion(bf16[96,1024]{1,0:T(8,128)(2,1)S(1)} %copy-done.6, f32[4096,192]{0,1:T(8,128)S(1)} %convert_element_type.67), kind=kOutput, calls=%fused_computation.24 | convolution fusion | flops 807665664 | bytes 20119552 | tf_op jit(solution)/shard_map/dot_general | solution.py:135
  180.2 0.6 copy-done.14
  181.0 339.7 %reduce-scatter.5.cloned.1.call-done = f32[64,1024]{1,0:T(8,128)} async-done(((f32[4096,1024]{1,0:T(8,128)}), f32[64,1024]{1,0:T(8,128)}) %reduce-scatter.5.cloned.1.call-update) | async-done | bytes 262160 | tf_op jit(solution)/shard_map/reduce_scatter | solution.py:134
  520.7 1.6 fusion.41
  522.4 81.9 %all_gather.7 = f32[1,131072]{1,0:T(1,128)S(1)} all-gather(f32[1,1024]{1,0:T(1,128)S(1)} %slice.36), channel_id=1, replica_groups=mesh['req'=64,'head'=2] {'req','head'}, dimensions={1}, use_global_device_ids=true | all-gather | bytes 528384 | tf_op jit(solution)/shard_map/all_gather | solution.py:143
  604.8 1.9 reduce.3
  606.9 4.2 fusion.44
  611.1 63.7 %pmax.7 = f32[64]{0:T(128)S(1)} all-reduce(f32[64]{0:T(128)S(1)} %get-tuple-element.14), channel_id=1, replica_groups=mesh['req'=64,'head'=2] {'req','head'}, use_global_device_ids=true, to_apply=%region_13.14 | all-reduce | flops 64 | bytes 512 | tf_op jit(solution)/shard_map/pmax | solution.py:146
  675.0 64.2 %psum.23 = f32[64]{0:T(128)S(1)} all-reduce(f32[64]{0:T(128)S(1)} %exponential_reduce_fusion), channel_id=1, replica_groups=mesh['req'=64,'head'=2] {'req','head'}, use_global_device_ids=true, to_apply=%region_15.16 | all-reduce | flops 64 | bytes 512 | tf_op jit(solution)/shard_map/psum | solution.py:147
  739.3 0.7 gather_fusion
  740.0 0.8 broadcast_select_fusion
  (76 shorter events, 3.8 us)
Async XLA Ops:
  7.2 15.3 %copy-start = (bf16[2048,512]{1,0:T(8,128)(2,1)S(1)}, bf16[2048,512]{1,0:T(8,128)(2,1)}, u32[]{:S(2)}) copy-start(bf16[2048,512]{1,0:T(8,128)(2,1)} %param.21) | copy-start | bytes 6291460
  7.2 10.9 %copy-start.10 = (f32[128]{0:T(128)S(1)}, f32[128]{0:T(128)}, u32[]{:S(2)}) copy-start(f32[128]{0:T(128)} %param.23) | copy-start | bytes 1540
  7.2 44.5 %reduce-scatter.3.cloned.1.call-start = ((), (), s32[]{:S(2)}) async-start(), calls=%async_computation.2 | async-start | bytes 393216 | tf_op jit(solution)/shard_map/reduce_scatter | solution.py:116
  17.7 4.8 copy-start.2
  17.7 4.8 copy-start.7
  18.4 4.8 copy-start.11
  23.0 4.6 copy-start.3
  28.1 3.6 copy-start.4
  33.6 21.6 %copy-start.9 = (f32[1024]{0:T(1024)S(1)}, f32[1024]{0:T(1024)}, u32[]{:S(2)}) copy-start(f32[1024]{0:T(1024)} %param.30) | copy-start | bytes 12292
  33.6 103.0 %copy-start.12 = (bf16[1024,96]{0,1:T(8,128)(2,1)S(1)}, bf16[1024,96]{0,1:T(8,128)(2,1)}, u32[]{:S(2)}) copy-start(bf16[1024,96]{0,1:T(8,128)(2,1)} %param.32) | copy-start | bytes 589828
  33.7 103.0 %copy-start.13 = (bf16[1024,96]{0,1:T(8,128)(2,1)S(1)}, bf16[1024,96]{0,1:T(8,128)(2,1)}, u32[]{:S(2)}) copy-start(bf16[1024,96]{0,1:T(8,128)(2,1)} %param.31) | copy-start | bytes 589828
  37.5 99.2 %all-gather.2.cloned.1.call-start = ((), (), s32[]{:S(2)}) async-start(), calls=%async_computation.3 | async-start | bytes 8519680 | tf_op jit(solution)/shard_map/all_gather | solution.py:125
  56.9 113.5 %all-reduce.2.cloned.1.call-start = ((), (), s32[]{:S(2)}) async-start(), calls=%async_computation.4 | async-start | bytes 3145728 | tf_op jit(solution)/shard_map/psum | solution.py:129
  144.2 27.9 %copy-start.6 = (bf16[96,1024]{1,0:T(8,128)(2,1)S(1)}, bf16[96,1024]{1,0:T(8,128)(2,1)}, u32[]{:S(2)}) copy-start(bf16[96,1024]{1,0:T(8,128)(2,1)} %param.33) | copy-start | bytes 589828
  144.2 376.5 %reduce-scatter.5.cloned.1.call-start = ((), (), s32[]{:S(2)}) async-start(), calls=%async_computation.5 | async-start | bytes 17039360 | tf_op jit(solution)/shard_map/reduce_scatter | solution.py:134
  180.2 0.7 copy-start.14
  180.2 340.5 %copy-start.5 = (bf16[64,1024]{1,0:T(8,128)(2,1)S(1)}, bf16[64,1024]{1,0:T(8,128)(2,1)}, u32[]{:S(2)}) copy-start(bf16[64,1024]{1,0:T(8,128)(2,1)} %reduce-scatter.3.cloned.1.call-done) | copy-start | bytes 393220
  180.9 426.0 %copy-start.8 = (f32[2048]{0:T(1024)S(1)}, f32[2048]{0:T(1024)}, u32[]{:S(2)}) copy-start(f32[2048]{0:T(1024)} %param.34) | copy-start | bytes 24580
  606.9 133.9 %copy-start.1 = (bf16[2048,512]{1,0:T(8,128)(2,1)S(1)}, bf16[2048,512]{1,0:T(8,128)(2,1)}, u32[]{:S(2)}) copy-start(bf16[2048,512]{1,0:T(8,128)(2,1)} %param.21) | copy-start | bytes 6291460
Sparse Core Ops, SparseCore 0:
  37.6 13.9 reduce-scatter.2
  57.0 79.6 all-gather.1
  144.3 25.9 all-reduce.1
  180.4 340.3 reduce-scatter.4
where the time goes:
time: 748 us; the launch traced here: 747 us
  waiting for transfers between devices  460 us (61%)
  blocking collectives  212 us (28%)
  matrix products  33.1 us (4%)
  between operations  16.1 us (2%)
  local copies, waits for them, and re-layouts  13.3 us (2%)
  other arithmetic  12.9 us (2%)
    reduce_scatter x1, waiting for transfers between devices, on_device(): lax.psum_scatter(jnp.dot(active, w_down, preferred_element_type=jnp.float...  340 us
    all_gather x1, blocking collectives, on_device(): lax.all_gather(last_row, ('req', 'head'), axis=1, tiled=True).reshape(-1, D)  81.9 us
    all_gather x1, waiting for transfers between devices, on_device(): lax.all_gather(mixed_rows, 'req', axis=0, tiled=True)  79.7 us
    psum x1, blocking collectives, on_device(): lax.psum(jnp.sum(jnp.exp(logits - row_max[:, None]), axis=1), ('req', 'he...  64.2 us
    pmax x1, blocking collectives, on_device(): row_max = lax.pmax(jnp.max(logits, axis=1), ('req', 'head'))  63.7 us
    psum x1, waiting for transfers between devices, on_device(): lax.psum(partial_rows.astype(jnp.bfloat16), 'head').astype(jnp.float32)  26.1 us
  transfers between devices with their start and end apart: 4, of which 4 were waited for; matrix products, arithmetic and copies ran while one was open for 0% of the time, Pallas kernels for 0%

commit v1 on v0

--- a/solution.py
+++ b/solution.py
@@ -144,7 +144,9 @@
     final_rows = norm_rows(collected, final_gain).astype(jnp.bfloat16)
     logits = jnp.dot(final_rows, w_vocab, preferred_element_type=jnp.float32)
     row_max = lax.pmax(jnp.max(logits, axis=1), ("req", "head"))
-    row_total = lax.psum(jnp.sum(jnp.exp(logits - row_max[:, None]), axis=1), ("req", "head"))
+    row_total = lax.psum(
+        lax.psum(jnp.sum(jnp.exp(logits - row_max[:, None]), axis=1), "head"), "req"
+    )
     log_probs = logits - row_max[:, None] - jnp.log(row_total)[:, None]
     log_probs = jnp.take(log_probs, inverse_order(slot_request), axis=0)
     return (hidden_out, log_probs)

time: 748 us -> 861 us (1.15)
  the two profiles are of different devices: /device:TPU:1 before, /device:TPU:0 now
where the time goes in v1:
time: 861 us; the launch traced here: 860 us
  waiting for transfers between devices  508 us (59%)
  blocking collectives  277 us (32%)
  matrix products  33.1 us (4%)
  between operations  16.1 us (2%)
  local copies, waits for them, and re-layouts  13.3 us (2%)
  other arithmetic  12.9 us (1%)
    reduce_scatter x1, waiting for transfers between devices, on_device(): lax.psum_scatter(jnp.dot(active, w_down, preferred_element_type=jnp.float...  389 us
    psum x1, blocking collectives, on_device(): lax.psum(lax.psum(jnp.sum(jnp.exp(logits - row_max[:, None]), axis=1), 'h...  175 us
    all_gather x1, waiting for transfers between devices, on_device(): lax.all_gather(mixed_rows, 'req', axis=0, tiled=True)  80.2 us
    pmax x1, blocking collectives, on_device(): row_max = lax.pmax(jnp.max(logits, axis=1), ('req', 'head'))  64 us
    all_gather x1, blocking collectives, on_device(): lax.all_gather(last_row, ('req', 'head'), axis=1, tiled=True).reshape(-1, D)  32.5 us
    psum x1, waiting for transfers between devices, on_device(): lax.psum(partial_rows.astype(jnp.bfloat16), 'head').astype(jnp.float32)  25.6 us
  transfers between devices with their start and end apart: 4, of which 4 were waited for; matrix products, arithmetic and copies ran while one was open for 0% of the time, Pallas kernels for 0%

profile of v1, /device:TPU:0, one launch (start us, length us, event | category | flops | bytes accessed | tf_op | source)
XLA Modules:
  0.0 860.1 jit_solution(697221007026178037)
XLA Ops:
  7.2 1.4 dynamic_slice.11
  10.6 1.2 dynamic_slice.12
  11.8 0.6 add_convert_fusion.2
  12.5 0.7 iota_compare_fusion.2
  13.2 1.1 multiply_reduce_fusion.1
  14.3 3.2 convolution_bitcast_fusion
  18.5 4.0 reshape.165
  23.5 4.1 reshape.167
  27.6 0.5 convolution_convert_fusion.2
  28.1 3.2 bitcast_reduce_fusion
  31.8 1.4 fusion.12
  33.7 3.8 convolution_convert_fusion.1
  37.6 12.7 %reduce-scatter.3.cloned.1.call-done = bf16[64,1024]{1,0:T(8,128)(2,1)} async-done(((bf16[64,2048]{1,0:T(8,128)(2,1)}), bf16[64,1024]{1,0:T(8,128)(2,1)}) %reduce-scatter.3.cloned.1.call-update) | async-done | bytes 131088 | tf_op jit(solution)/shard_map/reduce_scatter | solution.py:116
  50.3 1.0 multiply_reduce_fusion.2
  51.3 2.6 psum.28
  53.9 1.7 multiply_convert_fusion.3
  55.7 80.2 %all-gather.2.cloned.1.call-done = bf16[4096,1024]{1,0:T(8,128)(2,1)} async-done(((bf16[64,1024]{1,0:T(8,128)(2,1)}), bf16[4096,1024]{1,0:T(8,128)(2,1)}) %all-gather.2.cloned.1.call-update) | async-done | bytes 8388624 | tf_op jit(solution)/shard_map/all_gather | solution.py:125
  135.9 7.5 convolution_convert_fusion
  143.5 25.6 %all-reduce.2.cloned.1.call-done = bf16[4096,192]{0,1:T(8,128)(2,1)} async-done(((bf16[4096,192]{0,1:T(8,128)(2,1)}), bf16[4096,192]{0,1:T(8,128)(2,1)}) %all-reduce.2.cloned.1.call-update) | async-done | bytes 1572880 | tf_op jit(solution)/shard_map/psum | solution.py:129
  169.1 1.8 convert_element_type.67
  170.9 8.1 fusion.18
  179.0 0.6 copy-done.14
  179.8 389.0 %reduce-scatter.5.cloned.1.call-done = f32[64,1024]{1,0:T(8,128)} async-done(((f32[4096,1024]{1,0:T(8,128)}), f32[64,1024]{1,0:T(8,128)}) %reduce-scatter.5.cloned.1.call-update) | async-done | bytes 262160 | tf_op jit(solution)/shard_map/reduce_scatter | solution.py:134
  568.9 1.6 fusion.41
  570.5 32.5 %all_gather.7 = f32[1,131072]{1,0:T(1,128)S(1)} all-gather(f32[1,1024]{1,0:T(1,128)S(1)} %slice.36), channel_id=1, replica_groups=mesh['req'=64,'head'=2] {'req','head'}, dimensions={1}, use_global_device_ids=true | all-gather | bytes 528384 | tf_op jit(solution)/shard_map/all_gather | solution.py:143
  603.5 1.9 reduce.3
  605.6 4.2 fusion.44
  609.9 64.0 %pmax.7 = f32[64]{0:T(128)S(1)} all-reduce(f32[64]{0:T(128)S(1)} %get-tuple-element.14), channel_id=1, replica_groups=mesh['req'=64,'head'=2] {'req','head'}, use_global_device_ids=true, to_apply=%region_13.14 | all-reduce | flops 64 | bytes 512 | tf_op jit(solution)/shard_map/pmax | solution.py:146
  674.2 2.5 psum.30
  676.6 175.3 %psum.31 = f32[64]{0:T(128)S(1)} all-reduce(f32[64]{0:T(128)S(1)} %psum.30), channel_id=1, replica_groups=mesh['req'=64,'head'=2] {'req'}, use_global_device_ids=true, to_apply=%region_16.17 | all-reduce | flops 64 | bytes 512 | tf_op jit(solution)/shard_map/psum | solution.py:147
  852.0 0.7 gather_fusion
  852.7 0.8 broadcast_select_fusion
  (77 shorter events, 4.3 us)
Async XLA Ops:
  7.2 15.3 %copy-start = (bf16[2048,512]{1,0:T(8,128)(2,1)S(1)}, bf16[2048,512]{1,0:T(8,128)(2,1)}, u32[]{:S(2)}) copy-start(bf16[2048,512]{1,0:T(8,128)(2,1)} %param.21) | copy-start | bytes 6291460
  7.2 10.9 %copy-start.10 = (f32[128]{0:T(128)S(1)}, f32[128]{0:T(128)}, u32[]{:S(2)}) copy-start(f32[128]{0:T(128)} %param.23) | copy-start | bytes 1540
  7.2 43.1 %reduce-scatter.3.cloned.1.call-start = ((), (), s32[]{:S(2)}) async-start(), calls=%async_computation.2 | async-start | bytes 393216 | tf_op jit(solution)/shard_map/reduce_scatter | solution.py:116
  17.7 4.8 copy-start.2
  17.7 4.8 copy-start.7
  18.5 4.8 copy-start.11
  23.0 4.6 copy-start.3
  28.1 3.6 copy-start.4
  33.6 20.4 %copy-start.9 = (f32[1024]{0:T(1024)S(1)}, f32[1024]{0:T(1024)}, u32[]{:S(2)}) copy-start(f32[1024]{0:T(1024)} %param.30) | copy-start | bytes 12292
  33.6 102.3 %copy-start.12 = (bf16[1024,96]{0,1:T(8,128)(2,1)S(1)}, bf16[1024,96]{0,1:T(8,128)(2,1)}, u32[]{:S(2)}) copy-start(bf16[1024,96]{0,1:T(8,128)(2,1)} %param.32) | copy-start | bytes 589828
  33.7 102.2 %copy-start.13 = (bf16[1024,96]{0,1:T(8,128)(2,1)S(1)}, bf16[1024,96]{0,1:T(8,128)(2,1)}, u32[]{:S(2)}) copy-start(bf16[1024,96]{0,1:T(8,128)(2,1)} %param.31) | copy-start | bytes 589828
  37.5 98.4 %all-gather.2.cloned.1.call-start = ((), (), s32[]{:S(2)}) async-start(), calls=%async_computation.3 | async-start | bytes 8519680 | tf_op jit(solution)/shard_map/all_gather | solution.py:125
  55.6 113.5 %all-reduce.2.cloned.1.call-start = ((), (), s32[]{:S(2)}) async-start(), calls=%async_computation.4 | async-start | bytes 3145728 | tf_op jit(solution)/shard_map/psum | solution.py:129
  143.4 27.5 %copy-start.6 = (bf16[96,1024]{1,0:T(8,128)(2,1)S(1)}, bf16[96,1024]{1,0:T(8,128)(2,1)}, u32[]{:S(2)}) copy-start(bf16[96,1024]{1,0:T(8,128)(2,1)} %param.33) | copy-start | bytes 589828
  143.4 425.4 %reduce-scatter.5.cloned.1.call-start = ((), (), s32[]{:S(2)}) async-start(), calls=%async_computation.5 | async-start | bytes 17039360 | tf_op jit(solution)/shard_map/reduce_scatter | solution.py:134
  179.0 0.7 copy-start.14
  179.0 389.8 %copy-start.5 = (bf16[64,1024]{1,0:T(8,128)(2,1)S(1)}, bf16[64,1024]{1,0:T(8,128)(2,1)}, u32[]{:S(2)}) copy-start(bf16[64,1024]{1,0:T(8,128)(2,1)} %reduce-scatter.3.cloned.1.call-done) | copy-start | bytes 393220
  179.7 426.0 %copy-start.8 = (f32[2048]{0:T(1024)S(1)}, f32[2048]{0:T(1024)}, u32[]{:S(2)}) copy-start(f32[2048]{0:T(1024)} %param.34) | copy-start | bytes 24580
  605.6 247.9 %copy-start.1 = (bf16[2048,512]{1,0:T(8,128)(2,1)S(1)}, bf16[2048,512]{1,0:T(8,128)(2,1)}, u32[]{:S(2)}) copy-start(bf16[2048,512]{1,0:T(8,128)(2,1)} %param.21) | copy-start | bytes 6291460
Sparse Core Ops, SparseCore 0:
  37.6 12.6 reduce-scatter.2
  55.7 80.1 all-gather.1
  143.6 25.5 all-reduce.1
  179.2 389.6 reduce-scatter.4
